TPU v7x, 32 devices: a whole 2x2x4 slice. The times are simulated.
32 devices in a mesh: dp: 4 (over y, x), expert: 8 (over z, core).
Axes of the slice: x: 2, y: 2, z: 4, core: 2. Of those that a mesh axis runs over, the one named last changes fastest.
Arguments:
- tokens: bfloat16 [4096, 1536], P(('dp', 'expert')), may hold values from -6 to 6
- grad_out: bfloat16 [4096, 1536], P(('dp', 'expert')), may hold values from -6 to 6
- expert_ids: int32 [4096, 4], P(('dp', 'expert')), may hold values from 0 to 7, all different within a row; in each aligned block of 128 rows (0 to 127, 128 to 255, ...) at most 96 rows name the same one
- gate_q: int32 [4096, 4], P(('dp', 'expert')), may hold values from 1 to 65535
- w_up: bfloat16 [8, 1536, 768], P('expert', 'dp'), may hold values from -0.15625 to 0.15625
- w_down: bfloat16 [8, 768, 1536], P('expert', None, 'dp'), may hold values from -0.21875 to 0.21875
Outputs:
- dw_up: bfloat16 [8, 1536, 768], P('expert', 'dp')
- dw_down: bfloat16 [8, 768, 1536], P('expert', None, 'dp')
Inputs may be any that keep to these rules, and one draw needn't show every extreme that they name: `expert_ids`: within the rows of one device no expert is named by more than 96 rows, a bound that some block reaches; the 4 ids of a row differ.
All inputs are finite; a program needn't handle non-finite values.
Results may differ from a plain program's by a relative error of at most 0.0064.
Values may be sent and summed in bfloat16 or wider, within the bound.
No kernel may reach another device: no remote copies, remote signals or barrier semaphores. Data moves between devices by JAX's collectives and lax.ppermute only.
A program may use at most 64 MiB of HBM per device.

v0:
```python
import jax
import jax.numpy as jnp
from jax import lax
from jax.sharding import PartitionSpec as P


def silu_slope(values):
    sigmoid_part = jax.nn.sigmoid(values)
    return sigmoid_part * (1.0 + values * (1.0 - sigmoid_part))


def summed_up(recv_rows, projected_grad):
    first_dims = (((0,), (0,)), ((), ()))
    partial_value = lax.dot_general(
        recv_rows, projected_grad, first_dims, preferred_element_type=jnp.float32
    ).astype(jnp.bfloat16)
    pieces = lax.all_to_all(partial_value[None], "dp", split_axis=1, concat_axis=0, tiled=True)
    return jnp.sum(pieces.astype(jnp.float32), axis=0, keepdims=True).astype(jnp.bfloat16)


def summed_down(activated, grad_rows):
    first_dims = (((0,), (0,)), ((), ()))
    partial_value = lax.dot_general(
        activated, grad_rows, first_dims, preferred_element_type=jnp.float32
    ).astype(jnp.bfloat16)
    pieces = lax.all_to_all(partial_value[None], "dp", split_axis=2, concat_axis=0, tiled=True)
    return jnp.sum(pieces.astype(jnp.float32), axis=0, keepdims=True).astype(jnp.bfloat16)


def shards(tokens, grad_out, expert_ids, gate_q, w_up, w_down):
    devices = lax.axis_size("expert")
    token_count, top_count = expert_ids.shape
    model_width = tokens.shape[1]
    capacity = max(2, token_count * top_count * 3 // (2 * devices))
    slot_expert = expert_ids.reshape(-1)
    onehot_table = (slot_expert[:, None] == jnp.arange(devices, dtype=jnp.int32)[None, :]).astype(
        jnp.int32
    )
    earlier = jnp.cumsum(onehot_table, axis=0) - onehot_table
    slot_rank = jnp.sum(earlier * onehot_table, axis=1)
    slot_target = slot_expert * capacity + slot_rank
    gate_values = gate_q.reshape(-1).astype(jnp.float32) * (1.0 / 65536.0)
    token_rows = jnp.repeat(tokens, top_count, axis=0)
    slot_grads = (
        gate_values[:, None] * jnp.repeat(grad_out, top_count, axis=0).astype(jnp.float32)
    ).astype(jnp.bfloat16)
    empty_rows = jnp.zeros((devices * capacity, model_width), jnp.bfloat16)
    send_tokens = empty_rows.at[slot_target].set(token_rows).reshape(devices, capacity, model_width)
    grad_slots = empty_rows.at[slot_target].set(slot_grads).reshape(devices, capacity, model_width)
    contract_last = (((1,), (1,)), ((), ()))
    up_whole = lax.all_gather(w_up, "dp", axis=1, tiled=True)[0]
    down_whole = lax.all_gather(w_down, "dp", axis=2, tiled=True)[0]
    recv_tokens = lax.all_to_all(send_tokens, "expert", split_axis=0, concat_axis=0, tiled=True)
    recv_rows = recv_tokens.reshape(-1, model_width)
    projected = jnp.dot(recv_rows, up_whole, preferred_element_type=jnp.float32)
    recv_grads = lax.all_to_all(grad_slots, "expert", split_axis=0, concat_axis=0, tiled=True)
    activated = jax.nn.silu(projected).astype(jnp.bfloat16)
    grad_rows = recv_grads.reshape(-1, model_width)
    act_grad = lax.dot_general(
        grad_rows, down_whole, contract_last, preferred_element_type=jnp.float32
    )
    projected_grad = (act_grad * silu_slope(projected)).astype(jnp.bfloat16)
    up_grad = summed_up(recv_rows, projected_grad)
    down_grad = summed_down(activated, grad_rows)
    return (up_grad, down_grad)


def solution(mesh):
    in_specs = (
        P(("dp", "expert"), None),
        P(("dp", "expert"), None),
        P(("dp", "expert"), None),
        P(("dp", "expert"), None),
        P("expert", "dp", None),
        P("expert", None, "dp"),
    )
    out_specs = (P("expert", "dp", None), P("expert", None, "dp"))
    return jax.shard_map(shards, mesh=mesh, in_specs=in_specs, out_specs=out_specs, check_vma=False)
```

profile of v0, /device:TPU:0, one launch (start us, length us, event | category | flops | bytes accessed | tf_op | source)
XLA Modules:
  0.0 307.0 jit_solution(6901323254794781142)
XLA Ops:
  7.2 0.8 copy.25
  8.0 0.1 eq.29
  8.1 0.1 eq.25
  8.2 0.7 broadcast_multiply_fusion
  8.9 1.1 reduce-window.6
  10.0 0.2 slice_reduce_fusion
  10.2 0.1 copy.24
  10.4 0.1 mul.55
  10.5 1.4 broadcast_in_dim.22
  11.9 0.4 reshape.112
  12.3 0.1 fusion.17
  12.4 4.7 %scatter_custom_fusion = bf16[768,1536]{1,0:T(8,128)(2,1)} fusion(s32[512]{0:T(512)S(1)} %bitcast.53, bf16[512,1536]{1,0:T(8,128)(2,1)S(1)} %reshape.112, bf16[]{:T(256)} %constant.7.clone.1), kind=kCustom, calls=%fused_computation.18 | custom fusion | bytes 2359298 | tf_op jit(solution)/shard_map/scatter | solution.py:48
  17.1 6.5 %all-to-all-start = ((bf16[8,96,1536]{2,1,0:T(8,128)(2,1)}), bf16[8,96,1536]{2,1,0:T(8,128)(2,1)}, u32[]{:S(2)}, u32[]{:S(2)}) async-start(bf16[8,96,1536]{2,1,0:T(8,128)(2,1)} %bitcast.4), calls=%async_computation | async-start | bytes 4718592 | tf_op jit(solution)/shard_map/all_to_all | solution.py:53
  23.6 0.0 all-gather.5.cloned.1.call-start
  23.6 0.7 all-gather.5.cloned.1.call-update
  24.3 0.4 broadcast_in_dim.23
  24.7 2.3 convert_element_type.78
  27.0 0.1 copy.27
  27.1 0.1 mul.59
  27.2 6.0 %scatter_custom_fusion.1 = bf16[768,1536]{1,0:T(8,128)(2,1)} fusion(s32[512]{0:T(512)S(1)} %bitcast.54, f32[512,1536]{1,0:T(8,128)} %convert_element_type.78, f32[512]{0:T(512)S(1)} %mul.59, bf16[]{:T(256)} %constant.7.clone.1), kind=kCustom, calls=%fused_computation.14 | custom fusion | flops 1572864 | bytes 5507074 | tf_op jit(solution)/shard_map/scatter | solution.py:49
  33.3 45.1 %all-to-all-done = bf16[8,96,1536]{2,1,0:T(8,128)(2,1)} async-done(((bf16[8,96,1536]{2,1,0:T(8,128)(2,1)}), bf16[8,96,1536]{2,1,0:T(8,128)(2,1)}, u32[]{:S(2)}, u32[]{:S(2)}) %all-to-all-start) | async-done | bytes 2359328 | tf_op jit(solution)/shard_map/all_to_all | solution.py:53
  78.3 3.6 %all-to-all-start.1 = ((bf16[8,96,1536]{2,1,0:T(8,128)(2,1)}), bf16[8,96,1536]{2,1,0:T(8,128)(2,1)S(1)}, u32[]{:S(2)}, u32[]{:S(2)}) async-start(bf16[8,96,1536]{2,1,0:T(8,128)(2,1)} %bitcast.6), calls=%async_computation.1 | async-start | bytes 4718592 | tf_op jit(solution)/shard_map/all_to_all | solution.py:56
  81.9 0.2 all-gather.3.cloned.1.call-start
  82.2 0.5 all-gather.3.cloned.1.call-update
  82.7 0.0 all-gather.5.cloned.1.call-done
  82.7 5.8 %fusion.2 = f32[768,768]{1,0:T(8,128)} fusion(bf16[768,1536]{1,0:T(8,128)(2,1)} %bitcast.5, bf16[1,1536,768]{2,1,0:T(8,128)(2,1)} %all-gather.5.cloned.1.call-done), kind=kOutput, calls=%fused_computation.7 | convolution fusion | flops 1811939328 | bytes 7077888 | tf_op jit(solution)/shard_map/dot_general | solution.py:55
  88.5 34.7 %all-gather.3.cloned.1.call-done = bf16[1,768,1536]{2,1,0:T(8,128)(2,1)} async-done(((bf16[1,768,384]{2,1,0:T(8,128)(2,1)}), bf16[1,768,1536]{2,1,0:T(8,128)(2,1)}) %all-gather.3.cloned.1.call-update) | async-done | bytes 2359312 | tf_op jit(solution)/shard_map/all_gather | solution.py:52
  123.2 13.3 %all-to-all-done.1 = bf16[8,96,1536]{2,1,0:T(8,128)(2,1)S(1)} async-done(((bf16[8,96,1536]{2,1,0:T(8,128)(2,1)}), bf16[8,96,1536]{2,1,0:T(8,128)(2,1)S(1)}, u32[]{:S(2)}, u32[]{:S(2)}) %all-to-all-start.1) | async-done | bytes 2359328 | tf_op jit(solution)/shard_map/all_to_all | solution.py:56
  136.5 1.4 copy-done
  137.9 8.2 %fusion = bf16[1,1536,768]{2,1,0:T(8,128)(2,1)S(1)} fusion(bf16[768,1536]{1,0:T(8,128)(2,1)} %bitcast.5, f32[768,768]{1,0:T(8,128)} %fusion.2, bf16[768,1536]{1,0:T(8,128)(2,1)} %bitcast.48, bf16[1,768,1536]{2,1,0:T(8,128)(2,1)} %all-gather.3.cloned.1.call-done), kind=kOutput, calls=%fused_computation.5 | convolution fusion | flops 3630366720 | bytes 11796480 | tf_op jit(solution)/shard_map/dot_general | solution.py:14
  146.1 33.8 %copy.34 = bf16[1,1536,768]{2,0,1:T(2,128)(2,1)} copy(bf16[1,1536,768]{2,1,0:T(8,128)(2,1)S(1)} %fusion) | data formatting | bytes 4718592 | tf_op jit(solution)/shard_map/broadcast_in_dim | solution.py:17
  179.9 0.5 broadcast.72
  180.4 24.1 %reduce.7 = bf16[1536,768]{1,0:T(8,128)(2,1)S(1)} reduce(bf16[1536,1,768]{2,1,0:T(2,128)(2,1)} %bitcast.42, bf16[]{:T(256)} %broadcast.72), dimensions={1}, to_apply=%bitcast.41.reduce_sub_computation | reduce | bytes 4718594
  204.5 2.3 reshape.129
  206.8 3.9 %all-to-all-start.2 = ((bf16[4,2,147456]{2,1,0:T(2,128)(2,1)}), bf16[4,2,147456]{2,1,0:T(2,128)(2,1)S(1)}, u32[]{:S(2)}, u32[]{:S(2)}) async-start(bf16[4,2,147456]{2,1,0:T(2,128)(2,1)} %reshape.129), calls=%async_computation.2 | async-start | bytes 4718592 | tf_op jit(solution)/shard_map/all_to_all | solution.py:17
  210.6 5.9 %fusion.1 = bf16[1,768,1536]{2,1,0:T(8,128)(2,1)} fusion(bf16[768,1536]{1,0:T(8,128)(2,1)} %bitcast.49, f32[768,768]{1,0:T(8,128)} %fusion.2), kind=kOutput, calls=%fused_computation.6 | convolution fusion | flops 1816068096 | bytes 7077888 | tf_op jit(solution)/shard_map/dot_general | solution.py:23
  216.5 12.1 %copy.29 = bf16[1,768,1536]{1,0,2:T(2,128)(2,1)} copy(bf16[1,768,1536]{2,1,0:T(8,128)(2,1)} %fusion.1) | data formatting | bytes 4718592 | tf_op jit(solution)/shard_map/broadcast_in_dim | solution.py:26
  228.6 25.5 %reduce.8 = bf16[1536,768]{1,0:T(8,128)(2,1)} reduce(bf16[1536,1,768]{2,1,0:T(2,128)(2,1)} %bitcast.43, bf16[]{:T(256)} %broadcast.72), dimensions={1}, to_apply=%bitcast.34.reduce_sub_computation | reduce | bytes 4718594
  254.1 4.1 %reshape.131 = bf16[4,2,147456]{2,1,0:T(2,128)(2,1)} reshape(bf16[1536,768]{1,0:T(8,128)(2,1)} %reduce.8) | data formatting | bytes 4718592
  258.2 4.5 %all-to-all-start.3 = ((bf16[4,2,147456]{2,1,0:T(2,128)(2,1)}), bf16[4,2,147456]{2,1,0:T(2,128)(2,1)}, u32[]{:S(2)}, u32[]{:S(2)}) async-start(bf16[4,2,147456]{2,1,0:T(2,128)(2,1)} %reshape.131), calls=%async_computation.3 | async-start | bytes 4718592 | tf_op jit(solution)/shard_map/all_to_all | solution.py:26
  262.7 3.6 %reshape.130 = bf16[1536,1,768]{2,1,0:T(2,128)(2,1)} reshape(bf16[4,2,147456]{2,1,0:T(2,128)(2,1)S(1)} %all-to-all-done.2) | data formatting | bytes 4718592
  266.3 2.7 copy.31
  269.0 1.3 reduce.4
  270.3 20.1 %all-to-all-done.3 = bf16[4,2,147456]{2,1,0:T(2,128)(2,1)} async-done(((bf16[4,2,147456]{2,1,0:T(2,128)(2,1)}), bf16[4,2,147456]{2,1,0:T(2,128)(2,1)}, u32[]{:S(2)}, u32[]{:S(2)}) %all-to-all-start.3) | async-done | bytes 2359328 | tf_op jit(solution)/shard_map/all_to_all | solution.py:26
  290.5 5.2 %reshape.132 = bf16[1536,1,768]{2,1,0:T(2,128)(2,1)} reshape(bf16[4,2,147456]{2,1,0:T(2,128)(2,1)} %all-to-all-done.3) | data formatting | bytes 4718592
  295.6 2.7 copy.32
  298.4 0.7 reduce_sum.35
  299.1 1.1 copy.30
  (11 shorter events, 0.1 us)
Async XLA Ops:
  17.1 7.2 %copy-start.1 = (bf16[128,1536]{1,0:T(8,128)(2,1)S(1)}, bf16[128,1536]{1,0:T(8,128)(2,1)}, u32[]{:S(2)}) copy-start(bf16[128,1536]{1,0:T(8,128)(2,1)} %param.7) | copy-start | bytes 1179652
  17.1 61.2 %all-to-all-start = ((bf16[8,96,1536]{2,1,0:T(8,128)(2,1)}), bf16[8,96,1536]{2,1,0:T(8,128)(2,1)}, u32[]{:S(2)}, u32[]{:S(2)}) async-start(bf16[8,96,1536]{2,1,0:T(8,128)(2,1)} %bitcast.4), calls=%async_computation | async-start | bytes 4718592 | tf_op jit(solution)/shard_map/all_to_all | solution.py:53
  23.6 59.2 %all-gather.5.cloned.1.call-start = ((), (), s32[]{:S(2)}) async-start(), calls=%async_computation.5 | async-start | bytes 2949120 | tf_op jit(solution)/shard_map/all_gather | solution.py:51
  24.7 2.3 copy-start.2
  78.3 58.2 %all-to-all-start.1 = ((bf16[8,96,1536]{2,1,0:T(8,128)(2,1)}), bf16[8,96,1536]{2,1,0:T(8,128)(2,1)S(1)}, u32[]{:S(2)}, u32[]{:S(2)}) async-start(bf16[8,96,1536]{2,1,0:T(8,128)(2,1)} %bitcast.6), calls=%async_computation.1 | async-start | bytes 4718592 | tf_op jit(solution)/shard_map/all_to_all | solution.py:56
  81.9 41.3 %all-gather.3.cloned.1.call-start = ((), (), s32[]{:S(2)}) async-start(), calls=%async_computation.4 | async-start | bytes 2949120 | tf_op jit(solution)/shard_map/all_gather | solution.py:52
  136.5 1.4 copy-start
  206.8 51.5 %all-to-all-start.2 = ((bf16[4,2,147456]{2,1,0:T(2,128)(2,1)}), bf16[4,2,147456]{2,1,0:T(2,128)(2,1)S(1)}, u32[]{:S(2)}, u32[]{:S(2)}) async-start(bf16[4,2,147456]{2,1,0:T(2,128)(2,1)} %reshape.129), calls=%async_computation.2 | async-start | bytes 4718592 | tf_op jit(solution)/shard_map/all_to_all | solution.py:17
  258.2 32.2 %all-to-all-start.3 = ((bf16[4,2,147456]{2,1,0:T(2,128)(2,1)}), bf16[4,2,147456]{2,1,0:T(2,128)(2,1)}, u32[]{:S(2)}, u32[]{:S(2)}) async-start(bf16[4,2,147456]{2,1,0:T(2,128)(2,1)} %reshape.131), calls=%async_computation.3 | async-start | bytes 4718592 | tf_op jit(solution)/shard_map/all_to_all | solution.py:26
Sparse Core Ops, SparseCore 0:
  26.2 38.7 all-gather.4
  84.6 38.5 all-gather.2
where the time goes:
time: 308 us; the launch traced here: 307 us
  waiting for transfers between devices  114 us (37%)
  local copies, waits for them, and re-layouts  80.2 us (26%)
  other arithmetic  59.7 us (19%)
  matrix products  19.9 us (6%)
  starting transfers between devices  18.7 us (6%)
  between operations  14.2 us (5%)
    unnamed x2, other arithmetic  49.6 us
    all_to_all x1, waiting for transfers between devices, shards(): lax.all_to_all(send_tokens, 'expert', split_axis=0, concat_axis=0, tiled=...  45.1 us
    all_gather x1, waiting for transfers between devices, shards(): down_whole = lax.all_gather(w_down, 'dp', axis=2, tiled=True)[0]  34.7 us
    broadcast_in_dim x1, local copies, waits for them, and re-layouts, summed_up(): partial_value[None]  33.8 us
    unnamed x15, local copies, waits for them, and re-layouts  24.3 us
    all_to_all x1, waiting for transfers between devices, summed_down(): lax.all_to_all(partial_value[None], 'dp', split_axis=2, concat_axis=0, ti...  20.1 us
    all_to_all x1, waiting for transfers between devices, shards(): lax.all_to_all(grad_slots, 'expert', split_axis=0, concat_axis=0, tiled=T...  13.3 us
    broadcast_in_dim x1, local copies, waits for them, and re-layouts, summed_down(): partial_value[None]  12.1 us
  transfers between devices with their start and end apart: 6, of which 4 were waited for; matrix products, arithmetic and copies ran while one was open for 23% of the time, Pallas kernels for 0%

commit v1 on v0

--- a/solution.py
+++ b/solution.py
@@ -2,6 +2,18 @@
 import jax.numpy as jnp
 from jax import lax
 from jax.sharding import PartitionSpec as P
+
+
+def doubled_up(x, axis, dim):
+    ways, here, hop = (lax.axis_size(axis), lax.axis_index(axis), x.shape[dim])
+    line, have = (x, 1)
+    while have < ways:
+        line = jnp.concatenate(
+            [line, lax.ppermute(line, axis, [(d, (d - have) % ways) for d in range(ways)])],
+            axis=dim,
+        )
+        have = 2 * have
+    return jnp.roll(line, here * hop, axis=dim)
 
 
 def silu_slope(values):
@@ -49,7 +61,7 @@
     grad_slots = empty_rows.at[slot_target].set(slot_grads).reshape(devices, capacity, model_width)
     contract_last = (((1,), (1,)), ((), ()))
     up_whole = lax.all_gather(w_up, "dp", axis=1, tiled=True)[0]
-    down_whole = lax.all_gather(w_down, "dp", axis=2, tiled=True)[0]
+    down_whole = doubled_up(w_down, "dp", 2)[0]
     recv_tokens = lax.all_to_all(send_tokens, "expert", split_axis=0, concat_axis=0, tiled=True)
     recv_rows = recv_tokens.reshape(-1, model_width)
     projected = jnp.dot(recv_rows, up_whole, preferred_element_type=jnp.float32)

time: 308 us -> 324 us (1.052)
  waiting for transfers between devices: 114 us -> 120 us
  local copies, waits for them, and re-layouts: 80.2 us -> 85.2 us
  starting transfers between devices: 18.7 us -> 23.5 us
    ppermute x0 -> x2, waiting for transfers between devices: none -> 55 us  [doubled_up(): lax.ppermute(line, axis, [(d, (d - have) % ways) for d in range(ways)])]
    all_gather x1 -> x0, waiting for transfers between devices: 34.7 us -> none  [shards(): down_whole = lax.all_gather(w_down, 'dp', axis=2, tiled=True)[0]]
    all_to_all x1, waiting for transfers between devices: 13.3 us -> 0.01 us  [shards(): lax.all_to_all(grad_slots, 'expert', split_axis=0, concat_axis=0, tiled=T...]
    unnamed x15 -> x20, local copies, waits for them, and re-layouts: 24.3 us -> 27.9 us
  transfers between devices with their start and end apart: 6 -> 7, of which waited for: 4 -> 4; matrix products, arithmetic and copies ran while one was open for 23% -> 24% of each run, Pallas kernels for 0% -> 0%
where the time goes in v1:
time: 324 us; the launch traced here: 323 us
  waiting for transfers between devices  120 us (37%)
  local copies, waits for them, and re-layouts  85.2 us (26%)
  other arithmetic  59.8 us (18%)
  starting transfers between devices  23.5 us (7%)
  matrix products  20 us (6%)
  between operations  14.2 us (4%)
    ppermute x2, waiting for transfers between devices, doubled_up(): lax.ppermute(line, axis, [(d, (d - have) % ways) for d in range(ways)])  55 us
    unnamed x2, other arithmetic  49.7 us
    all_to_all x1, waiting for transfers between devices, shards(): lax.all_to_all(send_tokens, 'expert', split_axis=0, concat_axis=0, tiled=...  45.8 us
    broadcast_in_dim x1, local copies, waits for them, and re-layouts, summed_up(): partial_value[None]  34 us
    unnamed x20, local copies, waits for them, and re-layouts  27.9 us
    all_to_all x1, waiting for transfers between devices, summed_down(): lax.all_to_all(partial_value[None], 'dp', split_axis=2, concat_axis=0, ti...  18.6 us
    broadcast_in_dim x1, local copies, waits for them, and re-layouts, summed_down(): partial_value[None]  12.1 us
    dot_general x1, matrix products, summed_up(): lax.dot_general(recv_rows, projected_grad, first_dims, preferred_element_...  8.35 us
  transfers between devices with their start and end apart: 7, of which 4 were waited for; matrix products, arithmetic and copies ran while one was open for 24% of the time, Pallas kernels for 0%

profile of v1, /device:TPU:0, one launch (start us, length us, event | category | flops | bytes accessed | tf_op | source)
XLA Modules:
  0.0 322.6 jit_solution(16641994707311124458)
XLA Ops:
  7.2 0.8 copy.25
  8.1 0.1 eq.28
  8.2 0.7 broadcast_multiply_fusion
  8.9 1.1 reduce-window.6
  10.0 0.2 slice_reduce_fusion
  10.2 0.1 copy.24
  10.4 0.1 mul.58
  10.5 1.4 broadcast_in_dim.22
  11.9 0.4 reshape.112
  12.4 4.7 %scatter_custom_fusion = bf16[768,1536]{1,0:T(8,128)(2,1)} fusion(s32[512]{0:T(512)S(1)} %bitcast.51, bf16[512,1536]{1,0:T(8,128)(2,1)S(1)} %reshape.112, bf16[]{:T(256)} %constant.36.clone.1), kind=kCustom, calls=%fused_computation.20 | custom fusion | bytes 2359298 | tf_op jit(solution)/shard_map/scatter | solution.py:60
  17.1 6.5 %all-to-all-start = ((bf16[8,96,1536]{2,1,0:T(8,128)(2,1)}), bf16[8,96,1536]{2,1,0:T(8,128)(2,1)}, u32[]{:S(2)}, u32[]{:S(2)}) async-start(bf16[8,96,1536]{2,1,0:T(8,128)(2,1)} %bitcast.4), calls=%async_computation | async-start | bytes 4718592 | tf_op jit(solution)/shard_map/all_to_all | solution.py:65
  23.6 0.4 broadcast_in_dim.23
  24.0 2.3 convert_element_type.78
  26.3 0.1 copy.27
  26.4 0.1 mul.62
  26.5 6.1 %scatter_custom_fusion.1 = bf16[768,1536]{1,0:T(8,128)(2,1)} fusion(s32[512]{0:T(512)S(1)} %bitcast.52, f32[512,1536]{1,0:T(8,128)} %convert_element_type.78, f32[512]{0:T(512)S(1)} %mul.62, bf16[]{:T(256)} %constant.36.clone.1), kind=kCustom, calls=%fused_computation.15 | custom fusion | flops 1572864 | bytes 5507074 | tf_op jit(solution)/shard_map/scatter | solution.py:61
  32.6 45.8 %all-to-all-done = bf16[8,96,1536]{2,1,0:T(8,128)(2,1)} async-done(((bf16[8,96,1536]{2,1,0:T(8,128)(2,1)}), bf16[8,96,1536]{2,1,0:T(8,128)(2,1)}, u32[]{:S(2)}, u32[]{:S(2)}) %all-to-all-start) | async-done | bytes 2359328 | tf_op jit(solution)/shard_map/all_to_all | solution.py:65
  78.3 4.5 %all-to-all-start.1 = ((bf16[8,96,1536]{2,1,0:T(8,128)(2,1)}), bf16[8,96,1536]{2,1,0:T(8,128)(2,1)}, u32[]{:S(2)}, u32[]{:S(2)}) async-start(bf16[8,96,1536]{2,1,0:T(8,128)(2,1)} %bitcast.6), calls=%async_computation.1 | async-start | bytes 4718592 | tf_op jit(solution)/shard_map/all_to_all | solution.py:68
  82.9 0.7 all-gather.2.cloned.1.call-update
  83.6 2.7 collective-permute-start
  86.3 18.2 %collective-permute-done = bf16[1,768,384]{2,1,0:T(8,128)(2,1)S(1)} collective-permute-done((bf16[1,768,384]{2,1,0:T(8,128)(2,1)S(1)}, bf16[1,768,384]{2,1,0:T(8,128)(2,1)S(1)}, u32[]{:S(2)}, u32[]{:S(2)}) %collective-permute-start) | collective-permute-done | bytes 589856 | tf_op jit(solution)/shard_map/ppermute | solution.py:12
  104.6 1.0 constant_dynamic-update-slice_fusion.5
  105.6 1.0 constant_dynamic-update-slice_fusion.4
  106.6 36.8 %collective-permute-done.1 = bf16[1,768,768]{2,1,0:T(8,128)(2,1)S(1)} collective-permute-done((bf16[1,768,768]{2,1,0:T(8,128)(2,1)S(1)}, bf16[1,768,768]{2,1,0:T(8,128)(2,1)S(1)}, u32[]{:S(2)}, u32[]{:S(2)}) %collective-permute-start.1) | collective-permute-done | bytes 1179680 | tf_op jit(solution)/shard_map/ppermute | solution.py:12
  143.4 1.1 constant_dynamic-update-slice_fusion.3
  144.5 0.9 constant_dynamic-update-slice_fusion.2
  145.5 1.0 constant_dynamic-update-slice_fusion.1
  146.4 1.2 constant_dynamic-update-slice_fusion
  147.6 5.8 %fusion.2 = f32[768,768]{1,0:T(8,128)} fusion(bf16[768,1536]{1,0:T(8,128)(2,1)} %bitcast.5, bf16[1,1536,768]{2,1,0:T(8,128)(2,1)} %all-gather.2.cloned.1.call-done), kind=kOutput, calls=%fused_computation.7 | convolution fusion | flops 1811939328 | bytes 7077888 | tf_op jit(solution)/shard_map/dot_general | solution.py:67
  153.4 8.3 %fusion = bf16[1,1536,768]{2,1,0:T(8,128)(2,1)S(1)} fusion(bf16[768,1536]{1,0:T(8,128)(2,1)} %bitcast.5, f32[768,768]{1,0:T(8,128)} %fusion.2, bf16[768,1536]{1,0:T(8,128)(2,1)} %bitcast.7, bf16[1,768,3072]{2,1,0:T(8,128)(2,1)} %constant_dynamic-update-slice_fusion, s32[]{:T(128)S(6)} %select_n.26), kind=kOutput, calls=%fused_computation.5 | convolution fusion | flops 3630366720 | bytes 11796484 | tf_op jit(solution)/shard_map/dot_general | solution.py:26
  161.7 34.0 %copy.34 = bf16[1,1536,768]{2,0,1:T(2,128)(2,1)} copy(bf16[1,1536,768]{2,1,0:T(8,128)(2,1)S(1)} %fusion) | data formatting | bytes 4718592 | tf_op jit(solution)/shard_map/broadcast_in_dim | solution.py:29
  195.7 0.5 broadcast.72
  196.2 24.1 %reduce.7 = bf16[1536,768]{1,0:T(8,128)(2,1)S(1)} reduce(bf16[1536,1,768]{2,1,0:T(2,128)(2,1)} %bitcast.42, bf16[]{:T(256)} %broadcast.72), dimensions={1}, to_apply=%bitcast.41.reduce_sub_computation | reduce | bytes 4718594
  220.3 2.2 reshape.129
  222.6 5.2 %all-to-all-start.2 = ((bf16[4,2,147456]{2,1,0:T(2,128)(2,1)}), bf16[4,2,147456]{2,1,0:T(2,128)(2,1)S(1)}, u32[]{:S(2)}, u32[]{:S(2)}) async-start(bf16[4,2,147456]{2,1,0:T(2,128)(2,1)} %reshape.129), calls=%async_computation.2 | async-start | bytes 4718592 | tf_op jit(solution)/shard_map/all_to_all | solution.py:29
  227.8 5.8 %fusion.1 = bf16[1,768,1536]{2,1,0:T(8,128)(2,1)} fusion(bf16[768,1536]{1,0:T(8,128)(2,1)} %bitcast.7, f32[768,768]{1,0:T(8,128)} %fusion.2), kind=kOutput, calls=%fused_computation.6 | convolution fusion | flops 1816068096 | bytes 7077888 | tf_op jit(solution)/shard_map/dot_general | solution.py:35
  233.6 12.1 %copy.29 = bf16[1,768,1536]{1,0,2:T(2,128)(2,1)} copy(bf16[1,768,1536]{2,1,0:T(8,128)(2,1)} %fusion.1) | data formatting | bytes 4718592 | tf_op jit(solution)/shard_map/broadcast_in_dim | solution.py:38
  245.7 25.5 %reduce.8 = bf16[1536,768]{1,0:T(8,128)(2,1)} reduce(bf16[1536,1,768]{2,1,0:T(2,128)(2,1)} %bitcast.43, bf16[]{:T(256)} %broadcast.72), dimensions={1}, to_apply=%bitcast.34.reduce_sub_computation | reduce | bytes 4718594
  271.2 4.1 %reshape.131 = bf16[4,2,147456]{2,1,0:T(2,128)(2,1)} reshape(bf16[1536,768]{1,0:T(8,128)(2,1)} %reduce.8) | data formatting | bytes 4718592
  275.4 4.5 %all-to-all-start.3 = ((bf16[4,2,147456]{2,1,0:T(2,128)(2,1)}), bf16[4,2,147456]{2,1,0:T(2,128)(2,1)}, u32[]{:S(2)}, u32[]{:S(2)}) async-start(bf16[4,2,147456]{2,1,0:T(2,128)(2,1)} %reshape.131), calls=%async_computation.3 | async-start | bytes 4718592 | tf_op jit(solution)/shard_map/all_to_all | solution.py:38
  279.9 3.6 %reshape.130 = bf16[1536,1,768]{2,1,0:T(2,128)(2,1)} reshape(bf16[4,2,147456]{2,1,0:T(2,128)(2,1)S(1)} %all-to-all-done.2) | data formatting | bytes 4718592
  283.4 2.7 copy.31
  286.2 1.3 reduce.4
  287.5 18.6 %all-to-all-done.3 = bf16[4,2,147456]{2,1,0:T(2,128)(2,1)} async-done(((bf16[4,2,147456]{2,1,0:T(2,128)(2,1)}), bf16[4,2,147456]{2,1,0:T(2,128)(2,1)}, u32[]{:S(2)}, u32[]{:S(2)}) %all-to-all-start.3) | async-done | bytes 2359328 | tf_op jit(solution)/shard_map/all_to_all | solution.py:38
  306.1 5.2 %reshape.132 = bf16[1536,1,768]{2,1,0:T(2,128)(2,1)} reshape(bf16[4,2,147456]{2,1,0:T(2,128)(2,1)} %all-to-all-done.3) | data formatting | bytes 4718592
  311.3 2.7 copy.32
  314.0 0.7 reduce_sum.35
  314.7 1.1 copy.30
  (19 shorter events, 0.5 us)
Async XLA Ops:
  17.1 6.5 %copy-start.1 = (bf16[128,1536]{1,0:T(8,128)(2,1)S(1)}, bf16[128,1536]{1,0:T(8,128)(2,1)}, u32[]{:S(2)}) copy-start(bf16[128,1536]{1,0:T(8,128)(2,1)} %param.7) | copy-start | bytes 1179652
  17.1 61.2 %all-to-all-start = ((bf16[8,96,1536]{2,1,0:T(8,128)(2,1)}), bf16[8,96,1536]{2,1,0:T(8,128)(2,1)}, u32[]{:S(2)}, u32[]{:S(2)}) async-start(bf16[8,96,1536]{2,1,0:T(8,128)(2,1)} %bitcast.4), calls=%async_computation | async-start | bytes 4718592 | tf_op jit(solution)/shard_map/all_to_all | solution.py:65
  24.0 2.3 copy-start.2
  78.3 5.2 %copy-start = (bf16[1,768,384]{2,1,0:T(8,128)(2,1)S(1)}, bf16[1,768,384]{2,1,0:T(8,128)(2,1)}, u32[]{:S(2)}) copy-start(bf16[1,768,384]{2,1,0:T(8,128)(2,1)} %param.11) | copy-start | bytes 1769476
  78.3 75.0 %all-to-all-start.1 = ((bf16[8,96,1536]{2,1,0:T(8,128)(2,1)}), bf16[8,96,1536]{2,1,0:T(8,128)(2,1)}, u32[]{:S(2)}, u32[]{:S(2)}) async-start(bf16[8,96,1536]{2,1,0:T(8,128)(2,1)} %bitcast.6), calls=%async_computation.1 | async-start | bytes 4718592 | tf_op jit(solution)/shard_map/all_to_all | solution.py:68
  82.9 64.7 %all-gather.2.cloned.1.call-start = ((), (), s32[]{:S(2)}) async-start(), calls=%async_computation.4 | async-start | bytes 2949120 | tf_op jit(solution)/shard_map/all_gather | solution.py:63
  83.6 20.8 %collective-permute-start = (bf16[1,768,384]{2,1,0:T(8,128)(2,1)S(1)}, bf16[1,768,384]{2,1,0:T(8,128)(2,1)S(1)}, u32[]{:S(2)}, u32[]{:S(2)}) collective-permute-start(bf16[1,768,384]{2,1,0:T(8,128)(2,1)S(1)} %copy-done), channel_id=1, source_target_pairs={{0,24},{8,0},{16,8},{24,16},{1,25},{9,1},{17,9},{25,17},{2,26},{10... | collective-permute-start | bytes 1769480 | tf_op jit(solution)/shard_map/ppermute | solution.py:12
  104.5 38.9 %collective-permute-start.1 = (bf16[1,768,768]{2,1,0:T(8,128)(2,1)S(1)}, bf16[1,768,768]{2,1,0:T(8,128)(2,1)S(1)}, u32[]{:S(2)}, u32[]{:S(2)}) collective-permute-start(bf16[1,768,768]{2,1,0:T(8,128)(2,1)S(1)} %pad_maximum_fusion), channel_id=1, source_target_pairs={{0,16},{8,24},{16,0},{24,8},{1,17},{9,25},{17,1},{25,9},{2,18},{10... | collective-permute-start | bytes 3538952 | tf_op jit(solution)/shard_map/ppermute | solution.py:12
  222.6 52.8 %all-to-all-start.2 = ((bf16[4,2,147456]{2,1,0:T(2,128)(2,1)}), bf16[4,2,147456]{2,1,0:T(2,128)(2,1)S(1)}, u32[]{:S(2)}, u32[]{:S(2)}) async-start(bf16[4,2,147456]{2,1,0:T(2,128)(2,1)} %reshape.129), calls=%async_computation.2 | async-start | bytes 4718592 | tf_op jit(solution)/shard_map/all_to_all | solution.py:29
  275.4 30.7 %all-to-all-start.3 = ((bf16[4,2,147456]{2,1,0:T(2,128)(2,1)}), bf16[4,2,147456]{2,1,0:T(2,128)(2,1)}, u32[]{:S(2)}, u32[]{:S(2)}) async-start(bf16[4,2,147456]{2,1,0:T(2,128)(2,1)} %reshape.131), calls=%async_computation.3 | async-start | bytes 4718592 | tf_op jit(solution)/shard_map/all_to_all | solution.py:38
Sparse Core Ops, SparseCore 0:
  85.5 55.7 all-gather.1
